TPU v7x, 32 devices: a whole 2x2x4 slice. The times are simulated.
32 devices in a mesh: seq: 8 (over y, x, core), batch: 4 (over z).
Axes of the slice: x: 2, y: 2, z: 4, core: 2. Of those that a mesh axis runs over, the one named last changes fastest.
Arguments:
- stream_in: bfloat16 [16, 2048, 768], P('batch', 'seq'), may hold values from -6 to 6
- lengths: int32 [16], P('batch'), may hold values from 64 to 2048, as said below
- token_mask: int32 [16, 2048], P('batch', 'seq'), may hold values from 0 to 1, as said below
- norm1_gain: bfloat16 [768], replicated, may hold values from 0.5 to 1.5
- w_qkv: bfloat16 [768, 2304], replicated, may hold values from -0.21875 to 0.21875
- conv_taps: bfloat16 [3, 2304], replicated, may hold values from -3 to 3
- w_out: bfloat16 [768, 768], replicated, may hold values from -1.75 to 1.75
- norm2_gain: bfloat16 [768], replicated, may hold values from 0.5 to 1.5
- w_up: bfloat16 [768, 3072], replicated, may hold values from -0.21875 to 0.21875
- w_down: bfloat16 [3072, 768], replicated, may hold values from -0.109375 to 0.109375
- grad_output: bfloat16 [16, 2048, 768], P('batch', 'seq'), may hold values from -6 to 6
Outputs:
- stream_out: bfloat16 [16, 2048, 768], P('batch', 'seq')
- grad_input: float32 [16, 2048, 768], P('batch', 'seq')
- grad_norm1: float32 [768], P('batch')
- grad_qkv: float32 [768, 2304], P('batch')
- grad_taps: float32 [3, 2304], replicated
- grad_wout: float32 [768, 768], P('batch')
- grad_norm2: float32 [768], P('batch')
- grad_up: float32 [768, 3072], P('batch')
- grad_down: float32 [3072, 768], P('batch')
- block_rms: float32 [3], replicated
Inputs may be any that keep to these rules, and one draw needn't show every extreme that they name: `lengths`: lengths are heavy tailed over 64 to 2048; some sequence has exactly 2048. `token_mask`: 0 or 1; the first position of every sequence is 1.
All inputs are finite; a program needn't handle non-finite values.
Results may differ from a plain program's by a relative error of at most 0.02.
Values may be sent and summed in bfloat16 or wider, within the bound.
A program may use at most 384 MiB of HBM per device.

v0:
```python
import math
import jax
import jax.numpy as jnp
from jax import lax
from jax.sharding import PartitionSpec as P

HEADS = 12
HEAD = 64


def from_behind(value, axis, steps):
    count = lax.axis_size(axis)
    initial, last = (max(0, -steps), min(count, count - steps))
    return lax.ppermute(value, axis, [(source, source + steps) for source in range(initial, last)])


def dense(left_op, right_op):
    return jnp.dot(left_op, right_op, preferred_element_type=jnp.float32)


def norm_forward(values, gain_vec):
    factor = lax.rsqrt(jnp.mean(values * values, axis=-1, keepdims=True) + 1e-06)
    return (values * factor * gain_vec, factor)


def norm_backward(values, factor, gain_vec, upstream):
    weighted = upstream * gain_vec
    inner_mean = jnp.mean(weighted * values, axis=-1, keepdims=True)
    d_values = factor * weighted - values * (factor * factor * factor) * inner_mean
    d_gain = jnp.sum(upstream * values * factor, axis=(0, 1))
    return (d_values, d_gain)


def split_heads(row_block):
    return row_block.reshape(row_block.shape[0], HEADS, HEAD)


def score_block(q_rows, k_rows, q_begin, k_begin, length):
    factor = 1.0 / math.sqrt(HEAD)
    scores = (
        jnp.einsum(
            "qhe,khe->hqk",
            split_heads(q_rows),
            split_heads(k_rows),
            preferred_element_type=jnp.float32,
        )
        * factor
    )
    q_pos = q_begin + jnp.arange(q_rows.shape[0], dtype=jnp.int32)
    k_pos = k_begin + jnp.arange(k_rows.shape[0], dtype=jnp.int32)
    allowed = (k_pos[None, :] <= q_pos[:, None]) & (k_pos[None, :] < length)
    return (scores, allowed[None])


def attend_forward(q_rows, k_rows, v_rows, length, offset):
    scores, allowed = score_block(q_rows, k_rows, offset, 0, length)
    masked = jnp.where(allowed, scores, -1e30)
    row_max = jnp.max(masked, axis=-1, keepdims=True)
    exp_terms = jnp.exp(masked - row_max)
    row_total = jnp.sum(exp_terms, axis=-1, keepdims=True)
    weights = (exp_terms / row_total).astype(jnp.bfloat16)
    attended = jnp.einsum(
        "hqk,khe->qhe", weights, split_heads(v_rows), preferred_element_type=jnp.float32
    )
    return (attended.reshape(q_rows.shape[0], HEADS * HEAD), (row_max + jnp.log(row_total))[..., 0])


def attend_backward(q_rows, k_rows, v_rows, d_rows, log_total, length, offset):
    scores, allowed = score_block(q_rows, k_rows, offset, 0, length)
    prob_rows = jnp.where(allowed, jnp.exp(scores - log_total[..., None]), 0.0)
    d_probs = jnp.einsum(
        "qhe,khe->hqk", split_heads(d_rows), split_heads(v_rows), preferred_element_type=jnp.float32
    )
    delta_rows = jnp.sum(prob_rows * d_probs, axis=-1, keepdims=True)
    d_scores = (prob_rows * (d_probs - delta_rows)).astype(jnp.bfloat16)
    factor = 1.0 / math.sqrt(HEAD)
    d_query = (
        jnp.einsum(
            "hqk,khe->qhe", d_scores, split_heads(k_rows), preferred_element_type=jnp.float32
        ).reshape(q_rows.shape[0], HEADS * HEAD)
        * factor
    )
    return (d_query, d_scores, prob_rows, delta_rows[..., 0])


def shards(
    stream_in,
    lengths,
    token_mask,
    norm1_gain,
    w_qkv,
    conv_taps,
    w_out,
    norm2_gain,
    w_up,
    w_down,
    grad_output,
):
    seq_count, block_len, model_width = stream_in.shape
    offset = lax.axis_index("seq") * block_len
    factor = 1.0 / math.sqrt(HEAD)
    gain_one = norm1_gain.astype(jnp.float32)
    gain_two = norm2_gain.astype(jnp.float32)
    taps = conv_taps.astype(jnp.float32)
    resid = stream_in.astype(jnp.float32)
    positions = offset + jnp.arange(block_len, dtype=jnp.int32)
    stat_weight = token_mask.astype(jnp.float32) * (positions[None, :] < lengths[:, None]).astype(
        jnp.float32
    )
    cotangent = (grad_output.astype(jnp.float32) * stat_weight[..., None]).astype(jnp.bfloat16)
    normed1, factor_one = norm_forward(resid, gain_one)
    normed1_low = normed1.astype(jnp.bfloat16)
    projected = dense(normed1_low, w_qkv)
    rim_rows = from_behind(projected[:, block_len - 2 :], "seq", 1)
    extended = jnp.concatenate([rim_rows, projected], axis=1)
    mixed = (
        taps[0] * extended[:, 2:]
        + taps[1] * extended[:, 1 : block_len + 1]
        + taps[2] * extended[:, :block_len]
    ).astype(jnp.bfloat16)
    query = mixed[..., :model_width]
    keys_own = mixed[..., model_width : 2 * model_width]
    values_own = mixed[..., 2 * model_width :]
    keys_all, values_all = (
        lax.all_gather(keys_own, "seq", axis=1, tiled=True),
        lax.all_gather(values_own, "seq", axis=1, tiled=True),
    )

    def forward_one(item):
        return attend_forward(item[0], item[1], item[2], item[3], offset)

    attended, log_totals = lax.map(forward_one, (query, keys_all, values_all, lengths))
    attended_low = attended.astype(jnp.bfloat16)
    branch_attn = dense(attended_low, w_out)
    hidden1 = resid + branch_attn
    normed2, factor_two = norm_forward(hidden1, gain_two)
    normed2_low = normed2.astype(jnp.bfloat16)
    up_proj = dense(normed2_low, w_up)
    active = jax.nn.relu(up_proj)
    squared = (active * active).astype(jnp.bfloat16)
    branch_ff = dense(squared, w_down)
    stream_full = hidden1 + branch_ff
    stream_out = stream_full.astype(jnp.bfloat16)

    def masked_square(values):
        return jnp.sum(stat_weight * jnp.sum(values * values, axis=-1))

    local_stats = jnp.stack(
        [
            masked_square(stream_full),
            masked_square(branch_attn),
            masked_square(branch_ff),
            jnp.sum(stat_weight),
        ]
    )
    grad_down = jnp.einsum("scf,scd->fd", squared, cotangent, preferred_element_type=jnp.float32)
    d_squared = jnp.einsum("scd,fd->scf", cotangent, w_down, preferred_element_type=jnp.float32)
    d_up = (2.0 * active * d_squared).astype(jnp.bfloat16)
    grad_up = jnp.einsum("scd,scf->df", normed2_low, d_up, preferred_element_type=jnp.float32)
    d_normed2 = jnp.einsum("scf,df->scd", d_up, w_up, preferred_element_type=jnp.float32)
    d_hidden_norm, grad_norm2 = norm_backward(hidden1, factor_two, gain_two, d_normed2)
    d_hidden1 = cotangent.astype(jnp.float32) + d_hidden_norm
    d_attn = d_hidden1.astype(jnp.bfloat16)
    grad_wout = jnp.einsum("scd,sce->de", attended_low, d_attn, preferred_element_type=jnp.float32)
    d_attended = jnp.einsum(
        "sce,de->scd", d_attn, w_out, preferred_element_type=jnp.float32
    ).astype(jnp.bfloat16)

    def backward_local(item):
        d_query, d_scores, prob_rows, delta_rows = attend_backward(
            item[0], item[1], item[2], item[3], item[4], item[5], offset
        )
        return (d_query, delta_rows)

    d_query_all, delta_all = lax.map(
        backward_local, (query, keys_all, values_all, d_attended, log_totals, lengths)
    )
    lse_rows, delta_rows_all = (
        lax.all_gather(log_totals, "seq", axis=2, tiled=True),
        lax.all_gather(delta_all, "seq", axis=2, tiled=True),
    )
    begin_row = jnp.int32(0)
    q_piece = lax.all_gather(query, "seq", axis=1, tiled=True)
    d_piece = lax.all_gather(d_attended, "seq", axis=1, tiled=True)

    def per_sequence(q_rows, d_rows, k_rows, v_rows, lse_seq, delta_seq, length):
        scores, allowed = score_block(q_rows, k_rows, begin_row, offset, length)
        prob_rows = jnp.where(allowed, jnp.exp(scores - lse_seq[..., None]), 0.0)
        d_probs = jnp.einsum(
            "qhe,khe->hqk",
            split_heads(d_rows),
            split_heads(v_rows),
            preferred_element_type=jnp.float32,
        )
        d_scores = (prob_rows * (d_probs - delta_seq[..., None])).astype(jnp.bfloat16)
        d_keys_part = (
            jnp.einsum(
                "hqk,qhe->khe", d_scores, split_heads(q_rows), preferred_element_type=jnp.float32
            ).reshape(k_rows.shape[0], model_width)
            * factor
        )
        d_values_part = jnp.einsum(
            "hqk,qhe->khe",
            prob_rows.astype(jnp.bfloat16),
            split_heads(d_rows),
            preferred_element_type=jnp.float32,
        ).reshape(k_rows.shape[0], model_width)
        return (d_keys_part, d_values_part)

    d_keys_part, d_values_part = jax.vmap(per_sequence)(
        q_piece, d_piece, keys_own, values_own, lse_rows, delta_rows_all, lengths
    )
    d_mixed = jnp.concatenate([d_query_all, d_keys_part, d_values_part], axis=-1)
    rim_terms = jnp.stack(
        [taps[2] * d_mixed[:, 0], taps[1] * d_mixed[:, 0] + taps[2] * d_mixed[:, 1]], axis=1
    )
    back_rows = from_behind(rim_terms.astype(jnp.bfloat16), "seq", -1).astype(rim_terms.dtype)
    padded = jnp.concatenate(
        [d_mixed, jnp.zeros((seq_count, 2, 3 * model_width), jnp.float32)], axis=1
    )
    d_proj = (
        taps[0] * padded[:, :block_len]
        + taps[1] * padded[:, 1 : block_len + 1]
        + taps[2] * padded[:, 2:]
    )
    d_proj = d_proj + jnp.pad(back_rows, ((0, 0), (block_len - 2, 0), (0, 0)))
    d_proj_low = d_proj.astype(jnp.bfloat16)
    grad_taps = jnp.stack(
        [
            jnp.sum(d_mixed * extended[:, 2:], axis=(0, 1)),
            jnp.sum(d_mixed * extended[:, 1 : block_len + 1], axis=(0, 1)),
            jnp.sum(d_mixed * extended[:, :block_len], axis=(0, 1)),
        ]
    )
    grad_qkv = jnp.einsum(
        "scd,scn->dn", normed1_low, d_proj_low, preferred_element_type=jnp.float32
    )
    d_normed1 = jnp.einsum("scn,dn->scd", d_proj_low, w_qkv, preferred_element_type=jnp.float32)
    d_input_norm, grad_norm1 = norm_backward(resid, factor_one, gain_one, d_normed1)
    grad_input = d_hidden1 + d_input_norm
    shares = (
        lax.psum_scatter(
            grad_norm1.astype(jnp.bfloat16), "batch", scatter_dimension=0, tiled=True
        ).astype(jnp.float32),
        lax.psum_scatter(
            grad_qkv.astype(jnp.bfloat16), "batch", scatter_dimension=0, tiled=True
        ).astype(jnp.float32),
        lax.psum_scatter(
            grad_wout.astype(jnp.bfloat16), "batch", scatter_dimension=0, tiled=True
        ).astype(jnp.float32),
        lax.psum_scatter(
            grad_norm2.astype(jnp.bfloat16), "batch", scatter_dimension=0, tiled=True
        ).astype(jnp.float32),
        lax.psum_scatter(
            grad_up.astype(jnp.bfloat16), "batch", scatter_dimension=0, tiled=True
        ).astype(jnp.float32),
        lax.psum_scatter(
            grad_down.astype(jnp.bfloat16), "batch", scatter_dimension=0, tiled=True
        ).astype(jnp.float32),
    )
    totals = (
        lax.psum(shares[0].astype(jnp.bfloat16), "seq").astype(jnp.float32),
        lax.psum(shares[1].astype(jnp.bfloat16), "seq").astype(jnp.float32),
        lax.psum(shares[2].astype(jnp.bfloat16), "seq").astype(jnp.float32),
        lax.psum(shares[3].astype(jnp.bfloat16), "seq").astype(jnp.float32),
        lax.psum(shares[4].astype(jnp.bfloat16), "seq").astype(jnp.float32),
        lax.psum(shares[5].astype(jnp.bfloat16), "seq").astype(jnp.float32),
    )
    small = lax.psum((grad_taps, local_stats), ("seq", "batch"))
    block_rms = jnp.sqrt(small[1][:3] / (model_width * small[1][3]))
    return (
        stream_out,
        grad_input,
        totals[0],
        totals[1],
        small[0],
        totals[2],
        totals[3],
        totals[4],
        totals[5],
        block_rms,
    )


def solution(mesh):
    return jax.shard_map(
        shards,
        mesh=mesh,
        in_specs=(
            P("batch", "seq", None),
            P("batch"),
            P("batch", "seq"),
            P(),
            P(),
            P(),
            P(),
            P(),
            P(),
            P(),
            P("batch", "seq", None),
        ),
        out_specs=(
            P("batch", "seq", None),
            P("batch", "seq", None),
            P("batch"),
            P("batch", None),
            P(),
            P("batch", None),
            P("batch"),
            P("batch", None),
            P("batch", None),
            P(),
        ),
        check_vma=False,
    )
```

profile of v0, /device:TPU:0, one launch (start us, length us, event | category | flops | bytes accessed | tf_op | source)
XLA Modules:
  0.0 1237.5 jit_solution(3690341579583954142)
XLA Ops:
  23.6 13.4 %constant_dynamic-update-slice_fusion.1 = f32[4,258,2304]{2,0,1:T(4,128)} fusion(f32[4,258,2304]{2,0,1:T(4,128)} %constant_dynamic-update-slice_fusion.2, f32[4,256,2304]{2,1,0:T(8,128)} %copy-done.2), kind=kLoop, calls=%fused_computation.113 | loop fusion | bytes 18874368 | tf_op jit(solution)/shard_map/concatenate | solution.py:115
  37.0 17.5 %add_convert_fusion.1 = bf16[4,256,2304]{2,0,1:T(4,128)(2,1)S(1)} fusion(f32[4,258,2304]{2,0,1:T(4,128)} %constant_dynamic-update-slice_fusion.1, f32[2304]{0:T(1024)S(1)} %get-tuple-element.212, f32[2304]{0:T(1024)} %get-tuple-element.213, f32[2304]{0:T(1024)} %get-tuple-element.211, f32[4,256,2304]{2,1,0:T(8,128)} %copy-done.2), kind=kLoop, calls=%fused_computation.52 | loop fusion | flops 14155776 | bytes 33057792 | tf_op jit(solution)/shard_map/convert_element_type | solution.py:120
  64.8 70.0 %all-gather.7.cloned.1.call-done = bf16[4,2048,768]{2,0,1:T(4,128)(2,1)} async-done(((bf16[4,256,768]{2,0,1:T(4,128)(2,1)}), bf16[4,2048,768]{2,0,1:T(4,128)(2,1)}) %all-gather.7.cloned.1.call-update) | async-done | bytes 12582928 | tf_op jit(solution)/shard_map/all_gather | solution.py:125
  134.8 20.3 %copy.104 = bf16[4,2048,768]{1,2,0:T(8,128)(2,1)} copy(bf16[4,2048,768]{2,0,1:T(4,128)(2,1)} %all-gather.7.cloned.1.call-done) | data formatting | bytes 25165824 | tf_op jit(solution)/shard_map/while | solution.py:132
  155.1 53.8 %all-gather.5.cloned.1.call-done = bf16[4,2048,768]{2,0,1:T(4,128)(2,1)} async-done(((bf16[4,256,768]{2,0,1:T(4,128)(2,1)}), bf16[4,2048,768]{2,0,1:T(4,128)(2,1)}) %all-gather.5.cloned.1.call-update) | async-done | bytes 12582928 | tf_op jit(solution)/shard_map/all_gather | solution.py:126
  208.9 20.3 %copy.102 = bf16[4,2048,768]{1,2,0:T(8,128)(2,1)} copy(bf16[4,2048,768]{2,0,1:T(4,128)(2,1)} %all-gather.5.cloned.1.call-done) | data formatting | bytes 25165824 | tf_op jit(solution)/shard_map/while | solution.py:132
  229.8 170.0 %while.24 = (s32[]{:T(128)}, bf16[4,256,768]{1,2,0:T(8,128)(2,1)}, f32[4,12,256]{2,1,0:T(8,128)}, bf16[4,2048,768]{1,2,0:T(8,128)(2,1)}, s32[]{:T(128)}, /*index...) while((s32[]{:T(128)}, bf16[4,256,768]{1,2,0:T(8,128)(2,1)}, ...), condition=%wide.region_4.5_spmd, body=%wide.region_1.4_spmd.sunk | while | flops 1687158016 | bytes 98936960 | solution.py:132
  236.5 12.3 fusion.108
  260.5 12.0 fusion.110
  474.8 350.4 %while.25 = (s32[]{:T(128)}, f32[4,256,768]{2,0,1:T(4,128)}, f32[4,12,256]{2,1,0:T(8,128)}, bf16[4,2048,768]{1,2,0:T(8,128)(2,1)}, s32[]{:T(128)}, /*index=5*/s3...) while((s32[]{:T(128)}, f32[4,256,768]{2,0,1:T(4,128)}, ...), condition=%wide.region_9.10_spmd, body=%wide.region_7.9_spmd.sunk | while | flops 2486369536 | bytes 169195712 | solution.py:175
  502.7 19.8 %multiply_reduce_fusion.14 = (f32[12,256]{1,0:T(8,128)}, f32[12,256,2048]{2,1,0:T(8,128)}) fusion(f32[12,256,2048]{2,1,0:T(8,128)} %fusion.116, f32[12,256]{1,0:T(8,128)S(1)} %dynamic-slice_bitcast_fusion.2, pred[256,2048]{1,0:T(8,128)(4,1)} %fusion.117, bf16[256,12,64]{0,2,1:T(8,128)(2,1)} %bitcast.149, bf16[2048,12,64]{0,2,1:T(8,128)(2,1)} %bitcast.142), kind=kOutput, calls=%fused_computation.18.clone.1 | convolution fusion | flops 836760576 | bytes 54419456 | tf_op jit(solution)/shard_map/while/body/eval_jaxpr/qhe,khe->hqk/dot_general | solution.py:71
  522.5 20.4 %fusion.118 = f32[12,64,256]{2,1,0:T(8,128)} fusion(bf16[2048,12,64]{0,2,1:T(8,128)(2,1)} %bitcast.140, f32[12,256,2048]{2,1,0:T(8,128)} %get-tuple-element.413, f32[12,256,2048]{2,1,0:T(8,128)} %fusion.116, f32[12,256]{1,0:T(8,128)} %get-tuple-element.414, f32[12,256]{1,0:T(8,128)S(1)} %dynamic-slice_bitcast_fusion.2, pred[256,2048]{1,0:T(8,128)(4,1)} %fusion.117), kind=kOutput, calls=%fused_computation.24.clone.1 | convolution fusion | flops 843251712 | bytes 54812672 | tf_op jit(solution)/shard_map/while/body/eval_jaxpr/hqk,khe->qhe/dot_general | solution.py:78
  547.3 15.6 %dynamic_update_slice.24 = f32[4,256,768]{2,0,1:T(4,128)} dynamic-update-slice(f32[4,256,768]{2,0,1:T(4,128)} %get-tuple-element.455, f32[1,256,768]{2,0,1:T(1,128)} %copy.160, s32[]{:T(128)S(6)} %copy.178, s32[]{:T(128)} %constant.66.clone.1..sunk, s32[]{:T(128)} %constant.66.clone.1..sunk) | dynamic-update-slice | bytes 1572868 | tf_op jit(solution)/shard_map/while/body/jit(dynamic_update_index_in_dim)/dynamic_update_slice | solution.py:132
  590.6 19.8 %multiply_reduce_fusion.14 = (f32[12,256]{1,0:T(8,128)}, f32[12,256,2048]{2,1,0:T(8,128)}) fusion(f32[12,256,2048]{2,1,0:T(8,128)} %fusion.116, f32[12,256]{1,0:T(8,128)S(1)} %dynamic-slice_bitcast_fusion.2, pred[256,2048]{1,0:T(8,128)(4,1)} %fusion.117, bf16[256,12,64]{0,2,1:T(8,128)(2,1)} %bitcast.149, bf16[2048,12,64]{0,2,1:T(8,128)(2,1)} %bitcast.142), kind=kOutput, calls=%fused_computation.18.clone.1 | convolution fusion | flops 836760576 | bytes 54419456 | tf_op jit(solution)/shard_map/while/body/eval_jaxpr/qhe,khe->hqk/dot_general | solution.py:71
  610.4 20.3 %fusion.118 = f32[12,64,256]{2,1,0:T(8,128)} fusion(bf16[2048,12,64]{0,2,1:T(8,128)(2,1)} %bitcast.140, f32[12,256,2048]{2,1,0:T(8,128)} %get-tuple-element.413, f32[12,256,2048]{2,1,0:T(8,128)} %fusion.116, f32[12,256]{1,0:T(8,128)} %get-tuple-element.414, f32[12,256]{1,0:T(8,128)S(1)} %dynamic-slice_bitcast_fusion.2, pred[256,2048]{1,0:T(8,128)(4,1)} %fusion.117), kind=kOutput, calls=%fused_computation.24.clone.1 | convolution fusion | flops 843251712 | bytes 54812672 | tf_op jit(solution)/shard_map/while/body/eval_jaxpr/hqk,khe->qhe/dot_general | solution.py:78
  635.1 15.5 %dynamic_update_slice.24 = f32[4,256,768]{2,0,1:T(4,128)} dynamic-update-slice(f32[4,256,768]{2,0,1:T(4,128)} %get-tuple-element.455, f32[1,256,768]{2,0,1:T(1,128)} %copy.160, s32[]{:T(128)S(6)} %copy.178, s32[]{:T(128)} %constant.66.clone.1..sunk, s32[]{:T(128)} %constant.66.clone.1..sunk) | dynamic-update-slice | bytes 1572868 | tf_op jit(solution)/shard_map/while/body/jit(dynamic_update_index_in_dim)/dynamic_update_slice | solution.py:132
  678.2 19.8 %multiply_reduce_fusion.14 = (f32[12,256]{1,0:T(8,128)}, f32[12,256,2048]{2,1,0:T(8,128)}) fusion(f32[12,256,2048]{2,1,0:T(8,128)} %fusion.116, f32[12,256]{1,0:T(8,128)S(1)} %dynamic-slice_bitcast_fusion.2, pred[256,2048]{1,0:T(8,128)(4,1)} %fusion.117, bf16[256,12,64]{0,2,1:T(8,128)(2,1)} %bitcast.149, bf16[2048,12,64]{0,2,1:T(8,128)(2,1)} %bitcast.142), kind=kOutput, calls=%fused_computation.18.clone.1 | convolution fusion | flops 836760576 | bytes 54419456 | tf_op jit(solution)/shard_map/while/body/eval_jaxpr/qhe,khe->hqk/dot_general | solution.py:71
  697.9 20.1 %fusion.118 = f32[12,64,256]{2,1,0:T(8,128)} fusion(bf16[2048,12,64]{0,2,1:T(8,128)(2,1)} %bitcast.140, f32[12,256,2048]{2,1,0:T(8,128)} %get-tuple-element.413, f32[12,256,2048]{2,1,0:T(8,128)} %fusion.116, f32[12,256]{1,0:T(8,128)} %get-tuple-element.414, f32[12,256]{1,0:T(8,128)S(1)} %dynamic-slice_bitcast_fusion.2, pred[256,2048]{1,0:T(8,128)(4,1)} %fusion.117), kind=kOutput, calls=%fused_computation.24.clone.1 | convolution fusion | flops 843251712 | bytes 54812672 | tf_op jit(solution)/shard_map/while/body/eval_jaxpr/hqk,khe->qhe/dot_general | solution.py:78
  722.4 15.5 %dynamic_update_slice.24 = f32[4,256,768]{2,0,1:T(4,128)} dynamic-update-slice(f32[4,256,768]{2,0,1:T(4,128)} %get-tuple-element.455, f32[1,256,768]{2,0,1:T(1,128)} %copy.160, s32[]{:T(128)S(6)} %copy.178, s32[]{:T(128)} %constant.66.clone.1..sunk, s32[]{:T(128)} %constant.66.clone.1..sunk) | dynamic-update-slice | bytes 1572868 | tf_op jit(solution)/shard_map/while/body/jit(dynamic_update_index_in_dim)/dynamic_update_slice | solution.py:132
  765.5 19.8 %multiply_reduce_fusion.14 = (f32[12,256]{1,0:T(8,128)}, f32[12,256,2048]{2,1,0:T(8,128)}) fusion(f32[12,256,2048]{2,1,0:T(8,128)} %fusion.116, f32[12,256]{1,0:T(8,128)S(1)} %dynamic-slice_bitcast_fusion.2, pred[256,2048]{1,0:T(8,128)(4,1)} %fusion.117, bf16[256,12,64]{0,2,1:T(8,128)(2,1)} %bitcast.149, bf16[2048,12,64]{0,2,1:T(8,128)(2,1)} %bitcast.142), kind=kOutput, calls=%fused_computation.18.clone.1 | convolution fusion | flops 836760576 | bytes 54419456 | tf_op jit(solution)/shard_map/while/body/eval_jaxpr/qhe,khe->hqk/dot_general | solution.py:71
  785.2 20.1 %fusion.118 = f32[12,64,256]{2,1,0:T(8,128)} fusion(bf16[2048,12,64]{0,2,1:T(8,128)(2,1)} %bitcast.140, f32[12,256,2048]{2,1,0:T(8,128)} %get-tuple-element.413, f32[12,256,2048]{2,1,0:T(8,128)} %fusion.116, f32[12,256]{1,0:T(8,128)} %get-tuple-element.414, f32[12,256]{1,0:T(8,128)S(1)} %dynamic-slice_bitcast_fusion.2, pred[256,2048]{1,0:T(8,128)(4,1)} %fusion.117), kind=kOutput, calls=%fused_computation.24.clone.1 | convolution fusion | flops 843251712 | bytes 54812672 | tf_op jit(solution)/shard_map/while/body/eval_jaxpr/hqk,khe->qhe/dot_general | solution.py:78
  809.7 15.5 %dynamic_update_slice.24 = f32[4,256,768]{2,0,1:T(4,128)} dynamic-update-slice(f32[4,256,768]{2,0,1:T(4,128)} %get-tuple-element.455, f32[1,256,768]{2,0,1:T(1,128)} %copy.160, s32[]{:T(128)S(6)} %copy.178, s32[]{:T(128)} %constant.66.clone.1..sunk, s32[]{:T(128)} %constant.66.clone.1..sunk) | dynamic-update-slice | bytes 1572868 | tf_op jit(solution)/shard_map/while/body/jit(dynamic_update_index_in_dim)/dynamic_update_slice | solution.py:132
  857.3 20.1 %copy.110 = bf16[4,2048,768]{1,2,0:T(8,128)(2,1)} copy(bf16[4,2048,768]{2,0,1:T(4,128)(2,1)} %all-gather.9.cloned.1.call-done) | data formatting | bytes 25165824 | tf_op jit(solution)/shard_map/all_gather | solution.py:183
  877.5 39.7 %fusion.62 = f32[4,12,2048,256]{3,2,1,0:T(8,128)} fusion(bf16[4,2048,12,64]{1,3,2,0:T(8,128)(2,1)} %bitcast.147, bf16[4,256,12,64]{1,3,2,0:T(8,128)(2,1)} %bitcast.153), kind=kOutput, calls=%fused_computation.137 | convolution fusion | flops 3221225472 | bytes 114819072 | tf_op jit(solution)/shard_map/vmap(qhe,khe->hqk)/dot_general | solution.py:41
  917.2 16.0 %copy.112 = bf16[4,2048,768]{1,2,0:T(8,128)(2,1)} copy(bf16[4,2048,768]{2,1,0:T(8,128)(2,1)} %all-gather.11.cloned.1.call-done) | data formatting | bytes 25165824 | tf_op jit(solution)/shard_map/all_gather | solution.py:184
  933.2 38.9 %fusion.13 = f32[4,12,64,256]{3,2,1,0:T(8,128)} fusion(bf16[4,2048,12,64]{1,3,2,0:T(8,128)(2,1)} %bitcast.150, f32[4,12,2048,256]{3,2,1,0:T(8,128)} %fusion.62, f32[4,12,2048]{2,1,0:T(8,128)} %all_gather.21, pred[4,2048,256]{2,1,0:T(8,128)(4,1)} %broadcast_and_fusion), kind=kOutput, calls=%fused_computation.38 | convolution fusion | flops 3321888768 | bytes 118882304 | tf_op jit(solution)/shard_map/vmap(hqk,qhe->khe)/dot_general | solution.py:202
  977.1 51.0 %fusion.42 = f32[4,12,64,256]{3,2,1,0:T(8,128)} fusion(bf16[4,2048,12,64]{1,3,2,0:T(8,128)(2,1)} %bitcast.148, f32[4,12,2048,256]{3,2,1,0:T(8,128)} %fusion.62, f32[4,12,2048]{2,1,0:T(8,128)} %all_gather.23, f32[4,12,2048]{2,1,0:T(8,128)} %all_gather.21, pred[4,2048,256]{2,1,0:T(8,128)(4,1)} %broadcast_and_fusion, bf16[4,2048,12,64]{1,3,2,0:T(8,128)(2,1)} %bitcast.151, ...), kind=kOutput, calls=%fused_computation.94 | convolution fusion | flops 6594232320 | bytes 133431296 | tf_op jit(solution)/shard_map/vmap(hqk,qhe->khe)/dot_general | solution.py:197
  1033.0 20.5 %multiply_reduce_fusion.2 = (f32[2304]{0:T(1024)}, f32[2304]{0:T(1024)}, f32[2304]{0:T(1024)S(1)}, f32[4,256,2304]{2,0,1:T(4,128)S(1)}) fusion(f32[4,258,2304]{2,0,1:T(4,128)} %constant_dynamic-update-slice_fusion.1, f32[4,256,768]{2,0,1:T(4,128)} %copy.116, f32[4,256,768]{2,0,1:T(4,128)} %copy.115, f32[4,256,768]{2,0,1:T(4,128)} %get-tuple-element.108, ...), kind=kLoop, calls=%fused_computation.49 | loop fusion | flops 18867456 | bytes 47213568 | tf_op jit(solution)/shard_map/reduce_sum | solution.py:231
  1082.8 47.2 %all-reduce.4 = (f32[3,2304]{1,0:T(4,128)}, f32[4]{0:T(128)S(1)}) all-reduce(f32[3,2304]{1,0:T(4,128)} %pad_maximum_fusion.2, f32[4]{0:T(128)} %pad_maximum_fusion.3), channel_id=1, replica_groups=mesh['seq'=8,'batch'=4] {'seq','batch'}, use_global_device_ids=true, to_apply=%region_19.20 | all-reduce | flops 6916 | bytes 55328 | tf_op jit(solution)/shard_map/psum | solution.py:269
  1131.3 13.2 %reduce-scatter.5.cloned.1.call-done = bf16[192,2304]{1,0:T(8,128)(2,1)} async-done(((bf16[768,2304]{1,0:T(8,128)(2,1)}), bf16[192,2304]{1,0:T(8,128)(2,1)}) %reduce-scatter.5.cloned.1.call-update) | async-done | bytes 884752 | tf_op jit(solution)/shard_map/reduce_scatter | solution.py:245
  1167.7 12.5 %all-reduce.5 = (bf16[192]{0:T(256)(128)(2,1)}, bf16[192]{0:T(256)(128)(2,1)}) all-reduce(bf16[192]{0:T(256)(128)(2,1)S(1)} %dynamic-slice.1, bf16[192]{0:T(256)(128)(2,1)} %dynamic-slice.3), channel_id=1, replica_groups=mesh['seq'=8,'batch'=4] {'seq'}, use_global_device_ids=true, to_apply=%region_13.14 | all-reduce | flops 384 | bytes 1536 | tf_op jit(solution)/shard_map/psum | solution.py:262
  1188.3 34.7 %all-reduce.10.cloned.1.call-done = (bf16[192,2304]{1,0:T(8,128)(2,1)}, bf16[192,768]{1,0:T(8,128)(2,1)}, bf16[192,3072]{1,0:T(8,128)(2,1)}, bf16[768,768]{1,0:T(8,128)(2,1)}) async-done(((bf16[192,2304]{1,0:T(8,128)(2,1)}, bf16[192,768]{1,0:T(8,128)(2,1)}, bf16[192,3072]{1,0:T(8,128)(2,1)}, bf16[768,768]{1,0:T(8,128)(2,1)}), (bf16[192,2304]{1,0:T(8,128)(2,1)}, bf16[192,768]{1,0:T(8,128)(2,1)}, ...) | async-done | bytes 3538960 | tf_op jit(solution)/shard_map/psum | solution.py:263
  (259 shorter events, 485.8 us)
Async XLA Ops:
  7.2 127.6 %all-gather.7.cloned.1.call-start = ((), (), s32[]{:S(2)}) async-start(), calls=%async_computation.5 | async-start | bytes 14155776 | tf_op jit(solution)/shard_map/all_gather | solution.py:125
  8.1 8.0 copy-start.23
  10.7 5.4 copy-start.20
  10.7 11.6 copy-start.16
  19.7 3.3 collective-permute-start
  22.9 14.0 %copy-start.10 = (f32[2304]{0:T(1024)}, f32[2304]{0:T(1024)S(1)}, u32[]{:S(2)}) copy-start(f32[2304]{0:T(1024)S(1)} %get-tuple-element.212) | copy-start | bytes 27652
  57.4 151.4 %all-gather.5.cloned.1.call-start = ((), (), s32[]{:S(2)}) async-start(), calls=%async_computation.4 | async-start | bytes 14155776 | tf_op jit(solution)/shard_map/all_gather | solution.py:126
  58.2 799.2 %all-gather.9.cloned.1.call-start = ((), (), s32[]{:S(2)}) async-start(), calls=%async_computation.6 | async-start | bytes 14155776 | tf_op jit(solution)/shard_map/all_gather | solution.py:183
  64.5 852.7 %all-gather.11.cloned.1.call-start = ((), (), s32[]{:S(2)}) async-start(), calls=%async_computation.7 | async-start | bytes 14155776 | tf_op jit(solution)/shard_map/all_gather | solution.py:184
  399.8 13.6 %slice-start = ((s8[4718592]{0:T(1024)(128)(4,1)}), s8[4194304]{0:T(1024)(128)(4,1)S(1)}, s32[]{:S(2)}) async-start(s8[4718592]{0:T(1024)(128)(4,1)} %bitcast.157), calls=%async_computation.13 | async-start | bytes 8388608
  404.9 36.1 %copy-start.6 = (f32[4,256,768]{2,1,0:T(8,128)}, f32[4,256,768]{2,1,0:T(8,128)S(1)}, u32[]{:S(2)}) copy-start(f32[4,256,768]{2,1,0:T(8,128)S(1)} %get-tuple-element.267) | copy-start | bytes 9437188
  404.9 36.1 %copy-start.17 = (f32[4,256]{1,0:T(4,128)}, f32[4,256]{1,0:T(4,128)S(1)}, u32[]{:S(2)}) copy-start(f32[4,256]{1,0:T(4,128)S(1)} %get-tuple-element.287) | copy-start | bytes 12292
  404.9 8.5 copy-start.7
  404.9 8.5 copy-start.14
  404.9 8.5 slice-start.1
  446.4 684.8 %reduce-scatter.7.cloned.1.call-start = ((), (), s32[]{:S(2)}) async-start(), calls=%async_computation.9 | async-start | bytes 1474560 | tf_op jit(solution)/shard_map/reduce_scatter | solution.py:248
  452.5 678.8 %reduce-scatter.11.cloned.1.call-start = ((), (), s32[]{:S(2)}) async-start(), calls=%async_computation.11 | async-start | bytes 5898240 | tf_op jit(solution)/shard_map/reduce_scatter | solution.py:257
  474.1 657.1 %reduce-scatter.9.cloned.1.call-start = ((), (), s32[]{:S(2)}) async-start(), calls=%async_computation.10 | async-start | bytes 5898240 | tf_op jit(solution)/shard_map/reduce_scatter | solution.py:254
  857.3 287.2 %reduce-scatter.5.cloned.1.call-start = ((), (), s32[]{:S(2)}) async-start(), calls=%async_computation.8 | async-start | bytes 4423680 | tf_op jit(solution)/shard_map/reduce_scatter | solution.py:245
  1033.0 20.5 %copy-start.11 = (f32[2304]{0:T(1024)S(1)}, f32[2304]{0:T(1024)}, u32[]{:S(2)}) copy-start(f32[2304]{0:T(1024)} %copy-done.10) | copy-start | bytes 27652
  1033.0 20.5 %copy-start.12 = (f32[2304]{0:T(1024)S(1)}, f32[2304]{0:T(1024)}, u32[]{:S(2)}) copy-start(f32[2304]{0:T(1024)} %get-tuple-element.213) | copy-start | bytes 27652
  1033.0 24.4 %copy-start.13 = (f32[2304]{0:T(1024)S(1)}, f32[2304]{0:T(1024)}, u32[]{:S(2)}) copy-start(f32[2304]{0:T(1024)} %get-tuple-element.211) | copy-start | bytes 27652
  1053.6 15.0 %copy-start.4 = (bf16[4,256,768]{2,1,0:T(8,128)(2,1)S(1)}, bf16[4,256,768]{2,1,0:T(8,128)(2,1)}, u32[]{:S(2)}) copy-start(bf16[4,256,768]{2,1,0:T(8,128)(2,1)} %param.15) | copy-start | bytes 4718596
  1053.6 15.0 %copy-start.21 = (f32[4,256]{1,0:T(4,128)S(1)}, f32[4,256]{1,0:T(4,128)}, u32[]{:S(2)}) copy-start(f32[4,256]{1,0:T(4,128)} %copy-done.20) | copy-start | bytes 12292
  1053.6 15.0 %copy-start.24 = (f32[768]{0:T(1024)S(1)}, f32[768]{0:T(1024)}, u32[]{:S(2)}) copy-start(f32[768]{0:T(1024)} %copy-done.23) | copy-start | bytes 9220
  1053.7 3.8 collective-permute-start.1
  1074.2 148.8 %all-reduce.10.cloned.1.call-start = ((), (), s32[]{:S(2)}) async-start(), calls=%async_computation.12 | async-start | bytes 7077888 | tf_op jit(solution)/shard_map/psum | solution.py:263
  1077.5 67.5 %copy-start.22 = (f32[4,256]{1,0:T(4,128)S(1)}, f32[4,256]{1,0:T(4,128)}, u32[]{:S(2)}) copy-start(f32[4,256]{1,0:T(4,128)} %copy-done.20) | copy-start | bytes 12292
  1082.1 62.9 %copy-start.25 = (f32[768]{0:T(1024)S(1)}, f32[768]{0:T(1024)}, u32[]{:S(2)}) copy-start(f32[768]{0:T(1024)} %copy-done.23) | copy-start | bytes 9220
  1145.0 9.2 copy-start.31
  1145.0 38.4 %copy-start.19 = (f32[4,256]{1,0:T(4,128)S(1)}, f32[4,256]{1,0:T(4,128)}, u32[]{:S(2)}) copy-start(f32[4,256]{1,0:T(4,128)} %get-tuple-element.284) | copy-start | bytes 12292
  1223.0 6.1 copy-start.8
  (18 other events, 54.3 us)
Sparse Core Ops, SparseCore 0:
  57.5 77.2 all-gather.6
  136.7 72.1 all-gather.4
  210.8 72.1 all-gather.8
  446.5 72.1 all-gather.10
  520.9 29.1 reduce-scatter.6
  552.3 83.9 reduce-scatter.10
  857.4 85.4 reduce-scatter.8
  1074.3 70.0 reduce-scatter.4
  1148.1 74.8 all-reduce.9
where the time goes:
time: 1250 us; the launch traced here: 1240 us
  matrix products  510 us (41%)
  local copies, waits for them, and re-layouts  291 us (23%)
  waiting for transfers between devices  175 us (14%)
  other arithmetic  147 us (12%)
  blocking collectives  93.4 us (7%)
  between operations  15.8 us (1%)
    dot_general x9, matrix products, score_block(): jnp.einsum('qhe,khe->hqk', split_heads(q_rows), split_heads(k_rows), pref...  124 us
    dynamic_update_slice x16, local copies, waits for them, and re-layouts, shards(): lax.map(forward_one, (query, keys_all, values_all, lengths))  82.7 us
    dot_general x4, matrix products, attend_backward(): jnp.einsum('hqk,khe->qhe', d_scores, split_heads(k_rows), preferred_eleme...  81 us
    dot_general x4, matrix products, attend_backward(): jnp.einsum('qhe,khe->hqk', split_heads(d_rows), split_heads(v_rows), pref...  79.1 us
    all_gather x1, waiting for transfers between devices, shards(): lax.all_gather(keys_own, 'seq', axis=1, tiled=True)  70 us
    dynamic_slice x32, local copies, waits for them, and re-layouts, shards(): lax.map(forward_one, (query, keys_all, values_all, lengths))  68.3 us
    all_gather x1, waiting for transfers between devices, shards(): lax.all_gather(values_own, 'seq', axis=1, tiled=True)  53.8 us
    dot_general x1, matrix products, per_sequence(): jnp.einsum('hqk,qhe->khe', d_scores, split_heads(q_rows), preferred_eleme...  51 us
  transfers between devices with their start and end apart: 11, of which 5 were waited for; matrix products, arithmetic and copies ran while one was open for 71% of the time, Pallas kernels for 0%

commit v1 on v0

--- a/solution.py
+++ b/solution.py
@@ -266,7 +266,7 @@
         lax.psum(shares[4].astype(jnp.bfloat16), "seq").astype(jnp.float32),
         lax.psum(shares[5].astype(jnp.bfloat16), "seq").astype(jnp.float32),
     )
-    small = lax.psum((grad_taps, local_stats), ("seq", "batch"))
+    small = lax.psum(lax.psum((grad_taps, local_stats), "seq"), "batch")
     block_rms = jnp.sqrt(small[1][:3] / (model_width * small[1][3]))
     return (
         stream_out,

time: 1250 us -> 1250 us (level)
    psum x1 -> x2, blocking collectives: 47.2 us -> 52.1 us  [shards(): small = lax.psum(lax.psum((grad_taps, local_stats), 'seq'), 'batch')]
where the time goes in v1:
time: 1250 us; the launch traced here: 1240 us
  matrix products  510 us (41%)
  local copies, waits for them, and re-layouts  291 us (23%)
  waiting for transfers between devices  171 us (14%)
  other arithmetic  147 us (12%)
  blocking collectives  98.1 us (8%)
  between operations  15.8 us (1%)
    dot_general x9, matrix products, score_block(): jnp.einsum('qhe,khe->hqk', split_heads(q_rows), split_heads(k_rows), pref...  124 us
    dynamic_update_slice x16, local copies, waits for them, and re-layouts, shards(): lax.map(forward_one, (query, keys_all, values_all, lengths))  82.7 us
    dot_general x4, matrix products, attend_backward(): jnp.einsum('hqk,khe->qhe', d_scores, split_heads(k_rows), preferred_eleme...  81 us
    dot_general x4, matrix products, attend_backward(): jnp.einsum('qhe,khe->hqk', split_heads(d_rows), split_heads(v_rows), pref...  79.1 us
    all_gather x1, waiting for transfers between devices, shards(): lax.all_gather(keys_own, 'seq', axis=1, tiled=True)  70 us
    dynamic_slice x32, local copies, waits for them, and re-layouts, shards(): lax.map(forward_one, (query, keys_all, values_all, lengths))  68.3 us
    all_gather x1, waiting for transfers between devices, shards(): lax.all_gather(values_own, 'seq', axis=1, tiled=True)  53.8 us
    psum x2, blocking collectives, shards(): small = lax.psum(lax.psum((grad_taps, local_stats), 'seq'), 'batch')  52.1 us
  transfers between devices with their start and end apart: 11, of which 5 were waited for; matrix products, arithmetic and copies ran while one was open for 71% of the time, Pallas kernels for 0%

profile of v1, /device:TPU:0, one launch (start us, length us, event | category | flops | bytes accessed | tf_op | source)
XLA Modules:
  0.0 1237.9 jit_solution(437977196219980184)
XLA Ops:
  23.6 13.4 %constant_dynamic-update-slice_fusion.1 = f32[4,258,2304]{2,0,1:T(4,128)} fusion(f32[4,258,2304]{2,0,1:T(4,128)} %constant_dynamic-update-slice_fusion.2, f32[4,256,2304]{2,1,0:T(8,128)} %copy-done.2), kind=kLoop, calls=%fused_computation.113 | loop fusion | bytes 18874368 | tf_op jit(solution)/shard_map/concatenate | solution.py:115
  37.0 17.5 %add_convert_fusion.1 = bf16[4,256,2304]{2,0,1:T(4,128)(2,1)S(1)} fusion(f32[4,258,2304]{2,0,1:T(4,128)} %constant_dynamic-update-slice_fusion.1, f32[2304]{0:T(1024)S(1)} %get-tuple-element.212, f32[2304]{0:T(1024)} %get-tuple-element.213, f32[2304]{0:T(1024)} %get-tuple-element.211, f32[4,256,2304]{2,1,0:T(8,128)} %copy-done.2), kind=kLoop, calls=%fused_computation.52 | loop fusion | flops 14155776 | bytes 33057792 | tf_op jit(solution)/shard_map/convert_element_type | solution.py:120
  64.8 70.0 %all-gather.7.cloned.1.call-done = bf16[4,2048,768]{2,0,1:T(4,128)(2,1)} async-done(((bf16[4,256,768]{2,0,1:T(4,128)(2,1)}), bf16[4,2048,768]{2,0,1:T(4,128)(2,1)}) %all-gather.7.cloned.1.call-update) | async-done | bytes 12582928 | tf_op jit(solution)/shard_map/all_gather | solution.py:125
  134.8 20.3 %copy.104 = bf16[4,2048,768]{1,2,0:T(8,128)(2,1)} copy(bf16[4,2048,768]{2,0,1:T(4,128)(2,1)} %all-gather.7.cloned.1.call-done) | data formatting | bytes 25165824 | tf_op jit(solution)/shard_map/while | solution.py:132
  155.1 53.8 %all-gather.5.cloned.1.call-done = bf16[4,2048,768]{2,0,1:T(4,128)(2,1)} async-done(((bf16[4,256,768]{2,0,1:T(4,128)(2,1)}), bf16[4,2048,768]{2,0,1:T(4,128)(2,1)}) %all-gather.5.cloned.1.call-update) | async-done | bytes 12582928 | tf_op jit(solution)/shard_map/all_gather | solution.py:126
  208.9 20.3 %copy.102 = bf16[4,2048,768]{1,2,0:T(8,128)(2,1)} copy(bf16[4,2048,768]{2,0,1:T(4,128)(2,1)} %all-gather.5.cloned.1.call-done) | data formatting | bytes 25165824 | tf_op jit(solution)/shard_map/while | solution.py:132
  229.8 170.0 %while.24 = (s32[]{:T(128)}, bf16[4,256,768]{1,2,0:T(8,128)(2,1)}, f32[4,12,256]{2,1,0:T(8,128)}, bf16[4,2048,768]{1,2,0:T(8,128)(2,1)}, s32[]{:T(128)}, /*index...) while((s32[]{:T(128)}, bf16[4,256,768]{1,2,0:T(8,128)(2,1)}, ...), condition=%wide.region_4.5_spmd, body=%wide.region_1.4_spmd.sunk | while | flops 1687158016 | bytes 98936960 | solution.py:132
  236.5 12.3 fusion.108
  260.5 12.0 fusion.110
  474.8 350.4 %while.25 = (s32[]{:T(128)}, f32[4,256,768]{2,0,1:T(4,128)}, f32[4,12,256]{2,1,0:T(8,128)}, bf16[4,2048,768]{1,2,0:T(8,128)(2,1)}, s32[]{:T(128)}, /*index=5*/s3...) while((s32[]{:T(128)}, f32[4,256,768]{2,0,1:T(4,128)}, ...), condition=%wide.region_9.10_spmd, body=%wide.region_7.9_spmd.sunk | while | flops 2486369536 | bytes 169195712 | solution.py:175
  502.7 19.8 %multiply_reduce_fusion.14 = (f32[12,256]{1,0:T(8,128)}, f32[12,256,2048]{2,1,0:T(8,128)}) fusion(f32[12,256,2048]{2,1,0:T(8,128)} %fusion.116, f32[12,256]{1,0:T(8,128)S(1)} %dynamic-slice_bitcast_fusion.2, pred[256,2048]{1,0:T(8,128)(4,1)} %fusion.117, bf16[256,12,64]{0,2,1:T(8,128)(2,1)} %bitcast.149, bf16[2048,12,64]{0,2,1:T(8,128)(2,1)} %bitcast.142), kind=kOutput, calls=%fused_computation.18.clone.1 | convolution fusion | flops 836760576 | bytes 54419456 | tf_op jit(solution)/shard_map/while/body/eval_jaxpr/qhe,khe->hqk/dot_general | solution.py:71
  522.5 20.4 %fusion.118 = f32[12,64,256]{2,1,0:T(8,128)} fusion(bf16[2048,12,64]{0,2,1:T(8,128)(2,1)} %bitcast.140, f32[12,256,2048]{2,1,0:T(8,128)} %get-tuple-element.415, f32[12,256,2048]{2,1,0:T(8,128)} %fusion.116, f32[12,256]{1,0:T(8,128)} %get-tuple-element.416, f32[12,256]{1,0:T(8,128)S(1)} %dynamic-slice_bitcast_fusion.2, pred[256,2048]{1,0:T(8,128)(4,1)} %fusion.117), kind=kOutput, calls=%fused_computation.24.clone.1 | convolution fusion | flops 843251712 | bytes 54812672 | tf_op jit(solution)/shard_map/while/body/eval_jaxpr/hqk,khe->qhe/dot_general | solution.py:78
  547.3 15.6 %dynamic_update_slice.24 = f32[4,256,768]{2,0,1:T(4,128)} dynamic-update-slice(f32[4,256,768]{2,0,1:T(4,128)} %get-tuple-element.457, f32[1,256,768]{2,0,1:T(1,128)} %copy.160, s32[]{:T(128)S(6)} %copy.178, s32[]{:T(128)} %constant.66.clone.1..sunk, s32[]{:T(128)} %constant.66.clone.1..sunk) | dynamic-update-slice | bytes 1572868 | tf_op jit(solution)/shard_map/while/body/jit(dynamic_update_index_in_dim)/dynamic_update_slice | solution.py:132
  590.6 19.8 %multiply_reduce_fusion.14 = (f32[12,256]{1,0:T(8,128)}, f32[12,256,2048]{2,1,0:T(8,128)}) fusion(f32[12,256,2048]{2,1,0:T(8,128)} %fusion.116, f32[12,256]{1,0:T(8,128)S(1)} %dynamic-slice_bitcast_fusion.2, pred[256,2048]{1,0:T(8,128)(4,1)} %fusion.117, bf16[256,12,64]{0,2,1:T(8,128)(2,1)} %bitcast.149, bf16[2048,12,64]{0,2,1:T(8,128)(2,1)} %bitcast.142), kind=kOutput, calls=%fused_computation.18.clone.1 | convolution fusion | flops 836760576 | bytes 54419456 | tf_op jit(solution)/shard_map/while/body/eval_jaxpr/qhe,khe->hqk/dot_general | solution.py:71
  610.4 20.3 %fusion.118 = f32[12,64,256]{2,1,0:T(8,128)} fusion(bf16[2048,12,64]{0,2,1:T(8,128)(2,1)} %bitcast.140, f32[12,256,2048]{2,1,0:T(8,128)} %get-tuple-element.415, f32[12,256,2048]{2,1,0:T(8,128)} %fusion.116, f32[12,256]{1,0:T(8,128)} %get-tuple-element.416, f32[12,256]{1,0:T(8,128)S(1)} %dynamic-slice_bitcast_fusion.2, pred[256,2048]{1,0:T(8,128)(4,1)} %fusion.117), kind=kOutput, calls=%fused_computation.24.clone.1 | convolution fusion | flops 843251712 | bytes 54812672 | tf_op jit(solution)/shard_map/while/body/eval_jaxpr/hqk,khe->qhe/dot_general | solution.py:78
  635.1 15.5 %dynamic_update_slice.24 = f32[4,256,768]{2,0,1:T(4,128)} dynamic-update-slice(f32[4,256,768]{2,0,1:T(4,128)} %get-tuple-element.457, f32[1,256,768]{2,0,1:T(1,128)} %copy.160, s32[]{:T(128)S(6)} %copy.178, s32[]{:T(128)} %constant.66.clone.1..sunk, s32[]{:T(128)} %constant.66.clone.1..sunk) | dynamic-update-slice | bytes 1572868 | tf_op jit(solution)/shard_map/while/body/jit(dynamic_update_index_in_dim)/dynamic_update_slice | solution.py:132
  678.2 19.8 %multiply_reduce_fusion.14 = (f32[12,256]{1,0:T(8,128)}, f32[12,256,2048]{2,1,0:T(8,128)}) fusion(f32[12,256,2048]{2,1,0:T(8,128)} %fusion.116, f32[12,256]{1,0:T(8,128)S(1)} %dynamic-slice_bitcast_fusion.2, pred[256,2048]{1,0:T(8,128)(4,1)} %fusion.117, bf16[256,12,64]{0,2,1:T(8,128)(2,1)} %bitcast.149, bf16[2048,12,64]{0,2,1:T(8,128)(2,1)} %bitcast.142), kind=kOutput, calls=%fused_computation.18.clone.1 | convolution fusion | flops 836760576 | bytes 54419456 | tf_op jit(solution)/shard_map/while/body/eval_jaxpr/qhe,khe->hqk/dot_general | solution.py:71
  697.9 20.1 %fusion.118 = f32[12,64,256]{2,1,0:T(8,128)} fusion(bf16[2048,12,64]{0,2,1:T(8,128)(2,1)} %bitcast.140, f32[12,256,2048]{2,1,0:T(8,128)} %get-tuple-element.415, f32[12,256,2048]{2,1,0:T(8,128)} %fusion.116, f32[12,256]{1,0:T(8,128)} %get-tuple-element.416, f32[12,256]{1,0:T(8,128)S(1)} %dynamic-slice_bitcast_fusion.2, pred[256,2048]{1,0:T(8,128)(4,1)} %fusion.117), kind=kOutput, calls=%fused_computation.24.clone.1 | convolution fusion | flops 843251712 | bytes 54812672 | tf_op jit(solution)/shard_map/while/body/eval_jaxpr/hqk,khe->qhe/dot_general | solution.py:78
  722.4 15.5 %dynamic_update_slice.24 = f32[4,256,768]{2,0,1:T(4,128)} dynamic-update-slice(f32[4,256,768]{2,0,1:T(4,128)} %get-tuple-element.457, f32[1,256,768]{2,0,1:T(1,128)} %copy.160, s32[]{:T(128)S(6)} %copy.178, s32[]{:T(128)} %constant.66.clone.1..sunk, s32[]{:T(128)} %constant.66.clone.1..sunk) | dynamic-update-slice | bytes 1572868 | tf_op jit(solution)/shard_map/while/body/jit(dynamic_update_index_in_dim)/dynamic_update_slice | solution.py:132
  765.5 19.8 %multiply_reduce_fusion.14 = (f32[12,256]{1,0:T(8,128)}, f32[12,256,2048]{2,1,0:T(8,128)}) fusion(f32[12,256,2048]{2,1,0:T(8,128)} %fusion.116, f32[12,256]{1,0:T(8,128)S(1)} %dynamic-slice_bitcast_fusion.2, pred[256,2048]{1,0:T(8,128)(4,1)} %fusion.117, bf16[256,12,64]{0,2,1:T(8,128)(2,1)} %bitcast.149, bf16[2048,12,64]{0,2,1:T(8,128)(2,1)} %bitcast.142), kind=kOutput, calls=%fused_computation.18.clone.1 | convolution fusion | flops 836760576 | bytes 54419456 | tf_op jit(solution)/shard_map/while/body/eval_jaxpr/qhe,khe->hqk/dot_general | solution.py:71
  785.2 20.1 %fusion.118 = f32[12,64,256]{2,1,0:T(8,128)} fusion(bf16[2048,12,64]{0,2,1:T(8,128)(2,1)} %bitcast.140, f32[12,256,2048]{2,1,0:T(8,128)} %get-tuple-element.415, f32[12,256,2048]{2,1,0:T(8,128)} %fusion.116, f32[12,256]{1,0:T(8,128)} %get-tuple-element.416, f32[12,256]{1,0:T(8,128)S(1)} %dynamic-slice_bitcast_fusion.2, pred[256,2048]{1,0:T(8,128)(4,1)} %fusion.117), kind=kOutput, calls=%fused_computation.24.clone.1 | convolution fusion | flops 843251712 | bytes 54812672 | tf_op jit(solution)/shard_map/while/body/eval_jaxpr/hqk,khe->qhe/dot_general | solution.py:78
  809.7 15.5 %dynamic_update_slice.24 = f32[4,256,768]{2,0,1:T(4,128)} dynamic-update-slice(f32[4,256,768]{2,0,1:T(4,128)} %get-tuple-element.457, f32[1,256,768]{2,0,1:T(1,128)} %copy.160, s32[]{:T(128)S(6)} %copy.178, s32[]{:T(128)} %constant.66.clone.1..sunk, s32[]{:T(128)} %constant.66.clone.1..sunk) | dynamic-update-slice | bytes 1572868 | tf_op jit(solution)/shard_map/while/body/jit(dynamic_update_index_in_dim)/dynamic_update_slice | solution.py:132
  857.3 20.1 %copy.110 = bf16[4,2048,768]{1,2,0:T(8,128)(2,1)} copy(bf16[4,2048,768]{2,0,1:T(4,128)(2,1)} %all-gather.9.cloned.1.call-done) | data formatting | bytes 25165824 | tf_op jit(solution)/shard_map/all_gather | solution.py:183
  877.5 39.7 %fusion.62 = f32[4,12,2048,256]{3,2,1,0:T(8,128)} fusion(bf16[4,2048,12,64]{1,3,2,0:T(8,128)(2,1)} %bitcast.147, bf16[4,256,12,64]{1,3,2,0:T(8,128)(2,1)} %bitcast.153), kind=kOutput, calls=%fused_computation.137 | convolution fusion | flops 3221225472 | bytes 114819072 | tf_op jit(solution)/shard_map/vmap(qhe,khe->hqk)/dot_general | solution.py:41
  917.2 16.0 %copy.112 = bf16[4,2048,768]{1,2,0:T(8,128)(2,1)} copy(bf16[4,2048,768]{2,1,0:T(8,128)(2,1)} %all-gather.11.cloned.1.call-done) | data formatting | bytes 25165824 | tf_op jit(solution)/shard_map/all_gather | solution.py:184
  933.2 38.9 %fusion.13 = f32[4,12,64,256]{3,2,1,0:T(8,128)} fusion(bf16[4,2048,12,64]{1,3,2,0:T(8,128)(2,1)} %bitcast.150, f32[4,12,2048,256]{3,2,1,0:T(8,128)} %fusion.62, f32[4,12,2048]{2,1,0:T(8,128)} %all_gather.21, pred[4,2048,256]{2,1,0:T(8,128)(4,1)} %broadcast_and_fusion), kind=kOutput, calls=%fused_computation.38 | convolution fusion | flops 3321888768 | bytes 118882304 | tf_op jit(solution)/shard_map/vmap(hqk,qhe->khe)/dot_general | solution.py:202
  977.1 51.0 %fusion.42 = f32[4,12,64,256]{3,2,1,0:T(8,128)} fusion(bf16[4,2048,12,64]{1,3,2,0:T(8,128)(2,1)} %bitcast.148, f32[4,12,2048,256]{3,2,1,0:T(8,128)} %fusion.62, f32[4,12,2048]{2,1,0:T(8,128)} %all_gather.23, f32[4,12,2048]{2,1,0:T(8,128)} %all_gather.21, pred[4,2048,256]{2,1,0:T(8,128)(4,1)} %broadcast_and_fusion, bf16[4,2048,12,64]{1,3,2,0:T(8,128)(2,1)} %bitcast.151, ...), kind=kOutput, calls=%fused_computation.94 | convolution fusion | flops 6594232320 | bytes 133431296 | tf_op jit(solution)/shard_map/vmap(hqk,qhe->khe)/dot_general | solution.py:197
  1033.0 20.5 %multiply_reduce_fusion.2 = (f32[2304]{0:T(1024)}, f32[2304]{0:T(1024)}, f32[2304]{0:T(1024)S(1)}, f32[4,256,2304]{2,0,1:T(4,128)S(1)}) fusion(f32[4,258,2304]{2,0,1:T(4,128)} %constant_dynamic-update-slice_fusion.1, f32[4,256,768]{2,0,1:T(4,128)} %copy.116, f32[4,256,768]{2,0,1:T(4,128)} %copy.115, f32[4,256,768]{2,0,1:T(4,128)} %get-tuple-element.108, ...), kind=kLoop, calls=%fused_computation.49 | loop fusion | flops 18867456 | bytes 47213568 | tf_op jit(solution)/shard_map/reduce_sum | solution.py:231
  1082.8 26.9 %all-reduce.4 = (f32[3,2304]{1,0:T(4,128)}, f32[4]{0:T(128)S(1)}) all-reduce(f32[3,2304]{1,0:T(4,128)} %pad_maximum_fusion.2, f32[4]{0:T(128)} %pad_maximum_fusion.3), channel_id=1, replica_groups=mesh['seq'=8,'batch'=4] {'seq'}, use_global_device_ids=true, to_apply=%region_19.20 | all-reduce | flops 6916 | bytes 55328 | tf_op jit(solution)/shard_map/psum | solution.py:269
  1109.7 25.1 %all-reduce.5 = (f32[3,2304]{1,0:T(4,128)}, f32[4]{0:T(128)S(1)}) all-reduce(f32[3,2304]{1,0:T(4,128)} %get-tuple-element.254, f32[4]{0:T(128)S(1)} %get-tuple-element.255), channel_id=1, replica_groups=mesh['seq'=8,'batch'=4] {'batch'}, use_global_device_ids=true, to_apply=%region_20.21 | all-reduce | flops 6916 | bytes 55328 | tf_op jit(solution)/shard_map/psum | solution.py:269
  1168.1 12.6 %all-reduce.6 = (bf16[192]{0:T(256)(128)(2,1)}, bf16[192]{0:T(256)(128)(2,1)}) all-reduce(bf16[192]{0:T(256)(128)(2,1)S(1)} %dynamic-slice.1, bf16[192]{0:T(256)(128)(2,1)} %dynamic-slice.3), channel_id=1, replica_groups=mesh['seq'=8,'batch'=4] {'seq'}, use_global_device_ids=true, to_apply=%region_13.14 | all-reduce | flops 384 | bytes 1536 | tf_op jit(solution)/shard_map/psum | solution.py:262
  1188.8 34.7 %all-reduce.11.cloned.1.call-done = (bf16[192,2304]{1,0:T(8,128)(2,1)}, bf16[192,768]{1,0:T(8,128)(2,1)}, bf16[192,3072]{1,0:T(8,128)(2,1)}, bf16[768,768]{1,0:T(8,128)(2,1)}) async-done(((bf16[192,2304]{1,0:T(8,128)(2,1)}, bf16[192,768]{1,0:T(8,128)(2,1)}, bf16[192,3072]{1,0:T(8,128)(2,1)}, bf16[768,768]{1,0:T(8,128)(2,1)}), (bf16[192,2304]{1,0:T(8,128)(2,1)}, bf16[192,768]{1,0:T(8,128)(2,1)}, ...) | async-done | bytes 3538960 | tf_op jit(solution)/shard_map/psum | solution.py:263
  (260 shorter events, 494.5 us)
Async XLA Ops:
  7.2 127.6 %all-gather.7.cloned.1.call-start = ((), (), s32[]{:S(2)}) async-start(), calls=%async_computation.5 | async-start | bytes 14155776 | tf_op jit(solution)/shard_map/all_gather | solution.py:125
  8.1 8.0 copy-start.23
  10.7 5.4 copy-start.20
  10.7 11.6 copy-start.16
  19.7 3.3 collective-permute-start
  22.9 14.0 %copy-start.10 = (f32[2304]{0:T(1024)}, f32[2304]{0:T(1024)S(1)}, u32[]{:S(2)}) copy-start(f32[2304]{0:T(1024)S(1)} %get-tuple-element.212) | copy-start | bytes 27652
  57.4 151.4 %all-gather.5.cloned.1.call-start = ((), (), s32[]{:S(2)}) async-start(), calls=%async_computation.4 | async-start | bytes 14155776 | tf_op jit(solution)/shard_map/all_gather | solution.py:126
  58.2 799.2 %all-gather.9.cloned.1.call-start = ((), (), s32[]{:S(2)}) async-start(), calls=%async_computation.6 | async-start | bytes 14155776 | tf_op jit(solution)/shard_map/all_gather | solution.py:183
  64.5 852.7 %all-gather.11.cloned.1.call-start = ((), (), s32[]{:S(2)}) async-start(), calls=%async_computation.7 | async-start | bytes 14155776 | tf_op jit(solution)/shard_map/all_gather | solution.py:184
  399.8 13.6 %slice-start = ((s8[4718592]{0:T(1024)(128)(4,1)}), s8[4194304]{0:T(1024)(128)(4,1)S(1)}, s32[]{:S(2)}) async-start(s8[4718592]{0:T(1024)(128)(4,1)} %bitcast.157), calls=%async_computation.13 | async-start | bytes 8388608
  404.9 36.1 %copy-start.6 = (f32[4,256,768]{2,1,0:T(8,128)}, f32[4,256,768]{2,1,0:T(8,128)S(1)}, u32[]{:S(2)}) copy-start(f32[4,256,768]{2,1,0:T(8,128)S(1)} %get-tuple-element.269) | copy-start | bytes 9437188
  404.9 36.1 %copy-start.17 = (f32[4,256]{1,0:T(4,128)}, f32[4,256]{1,0:T(4,128)S(1)}, u32[]{:S(2)}) copy-start(f32[4,256]{1,0:T(4,128)S(1)} %get-tuple-element.289) | copy-start | bytes 12292
  404.9 8.5 copy-start.7
  404.9 8.5 copy-start.14
  404.9 8.5 slice-start.1
  446.4 689.7 %reduce-scatter.7.cloned.1.call-start = ((), (), s32[]{:S(2)}) async-start(), calls=%async_computation.9 | async-start | bytes 1474560 | tf_op jit(solution)/shard_map/reduce_scatter | solution.py:248
  452.5 683.6 %reduce-scatter.11.cloned.1.call-start = ((), (), s32[]{:S(2)}) async-start(), calls=%async_computation.11 | async-start | bytes 5898240 | tf_op jit(solution)/shard_map/reduce_scatter | solution.py:257
  474.1 662.0 %reduce-scatter.9.cloned.1.call-start = ((), (), s32[]{:S(2)}) async-start(), calls=%async_computation.10 | async-start | bytes 5898240 | tf_op jit(solution)/shard_map/reduce_scatter | solution.py:254
  857.3 287.8 %reduce-scatter.5.cloned.1.call-start = ((), (), s32[]{:S(2)}) async-start(), calls=%async_computation.8 | async-start | bytes 4423680 | tf_op jit(solution)/shard_map/reduce_scatter | solution.py:245
  1033.0 20.5 %copy-start.11 = (f32[2304]{0:T(1024)S(1)}, f32[2304]{0:T(1024)}, u32[]{:S(2)}) copy-start(f32[2304]{0:T(1024)} %copy-done.10) | copy-start | bytes 27652
  1033.0 20.5 %copy-start.12 = (f32[2304]{0:T(1024)S(1)}, f32[2304]{0:T(1024)}, u32[]{:S(2)}) copy-start(f32[2304]{0:T(1024)} %get-tuple-element.213) | copy-start | bytes 27652
  1033.0 24.4 %copy-start.13 = (f32[2304]{0:T(1024)S(1)}, f32[2304]{0:T(1024)}, u32[]{:S(2)}) copy-start(f32[2304]{0:T(1024)} %get-tuple-element.211) | copy-start | bytes 27652
  1053.6 15.0 %copy-start.4 = (bf16[4,256,768]{2,1,0:T(8,128)(2,1)S(1)}, bf16[4,256,768]{2,1,0:T(8,128)(2,1)}, u32[]{:S(2)}) copy-start(bf16[4,256,768]{2,1,0:T(8,128)(2,1)} %param.15) | copy-start | bytes 4718596
  1053.6 15.0 %copy-start.21 = (f32[4,256]{1,0:T(4,128)S(1)}, f32[4,256]{1,0:T(4,128)}, u32[]{:S(2)}) copy-start(f32[4,256]{1,0:T(4,128)} %copy-done.20) | copy-start | bytes 12292
  1053.6 15.0 %copy-start.24 = (f32[768]{0:T(1024)S(1)}, f32[768]{0:T(1024)}, u32[]{:S(2)}) copy-start(f32[768]{0:T(1024)} %copy-done.23) | copy-start | bytes 9220
  1053.7 3.8 collective-permute-start.1
  1074.2 149.3 %all-reduce.11.cloned.1.call-start = ((), (), s32[]{:S(2)}) async-start(), calls=%async_computation.12 | async-start | bytes 7077888 | tf_op jit(solution)/shard_map/psum | solution.py:263
  1077.5 68.1 %copy-start.22 = (f32[4,256]{1,0:T(4,128)S(1)}, f32[4,256]{1,0:T(4,128)}, u32[]{:S(2)}) copy-start(f32[4,256]{1,0:T(4,128)} %copy-done.20) | copy-start | bytes 12292
  1082.1 63.5 %copy-start.25 = (f32[768]{0:T(1024)S(1)}, f32[768]{0:T(1024)}, u32[]{:S(2)}) copy-start(f32[768]{0:T(1024)} %copy-done.23) | copy-start | bytes 9220
  1145.6 9.2 copy-start.31
  1145.6 38.3 %copy-start.19 = (f32[4,256]{1,0:T(4,128)S(1)}, f32[4,256]{1,0:T(4,128)}, u32[]{:S(2)}) copy-start(f32[4,256]{1,0:T(4,128)} %get-tuple-element.286) | copy-start | bytes 12292
  1223.5 6.1 copy-start.8
  (18 other events, 54.3 us)
Sparse Core Ops, SparseCore 0:
  57.5 77.2 all-gather.6
  136.7 72.1 all-gather.4
  210.8 72.1 all-gather.8
  446.5 72.1 all-gather.10
  520.9 29.1 reduce-scatter.6
  552.3 83.9 reduce-scatter.10
  857.4 85.4 reduce-scatter.8
  1074.3 70.6 reduce-scatter.4
  1148.7 74.6 all-reduce.10
